TPU v7x, 128 devices: a whole 4x4x4 slice. The times are simulated.
128 devices in a mesh: dp: 4 (over x), fsdp: 32 (over z, y, core).
Axes of the slice: x: 4, y: 4, z: 4, core: 2. Of those that a mesh axis runs over, the one named last changes fastest.
Arguments:
- mlp_input: bfloat16 [1024, 4096], P('dp', 'fsdp'), may hold values from -6 to 6
- residual_in: bfloat16 [1024, 4096], P(('dp', 'fsdp')), may hold values from -6 to 6
- gate_weight: bfloat16 [4096, 14336], P(None, 'fsdp'), may hold values from -0.09375 to 0.09375
- up_weight: bfloat16 [4096, 14336], P(None, 'fsdp'), may hold values from -0.09375 to 0.09375
- down_weight: bfloat16 [14336, 4096], P('fsdp'), may hold values from -0.046875 to 0.046875
- span_index: bfloat16 [65536, 4096], P(('dp', 'fsdp')), may hold values from -6 to 6
- positive_keys: bfloat16 [1024, 4096], P(('dp', 'fsdp')), may hold values from -6 to 6
- request_rows: int32 [128, 128, 8], P(None, ('dp', 'fsdp')), may hold values from 0 to 511, as said below
- request_counts: int32 [128, 128], P(None, ('dp', 'fsdp')), may hold values from 0 to 8, as said below
- negative_slots: int32 [1024, 64], P(('dp', 'fsdp')), may hold values from 0 to 1023, as said below
Outputs:
- query_loss: float32 [1024], P(('dp', 'fsdp'))
- input_grad: bfloat16 [1024, 4096], P('dp', 'fsdp')
- gate_grad: bfloat16 [4096, 14336], P('dp', 'fsdp')
- up_grad: bfloat16 [4096, 14336], P('dp', 'fsdp')
- down_grad: bfloat16 [14336, 4096], P('fsdp', 'dp')
Inputs may be any that keep to these rules, and one draw needn't show every extreme that they name: `request_rows`: entry [r, o, s] is a local row of shard o; it is read only where s < request_counts[r, o]. `request_counts`: for each requesting device r the counts over the 128 shards sum to 512, and some shard gets exactly 8. `negative_slots`: rows q of device r = q // 8; an entry o * 8 + s names slot s of shard o with s < request_counts[r, o]; the 512 entries of a device use each such slot exactly once.
All inputs are finite; a program needn't handle non-finite values.
Results may differ from a plain program's by a relative error of at most 0.017.
Values may be sent and summed in bfloat16 or wider, within the bound.
A program may use at most 128 MiB of HBM per device.

v0:
```python
import jax
import jax.numpy as jnp
from jax import lax
from jax.sharding import PartitionSpec as P

inverse_temp = 50.0
eps = 1e-06
contract_first = (((0,), (0,)), ((), ()))
contract_last = (((1,), (1,)), ((), ()))


def split3(v):
    hi = lax.reduce_precision(v, 8, 7)
    mid = lax.reduce_precision(v - hi, 8, 7)
    return jnp.concatenate([hi, mid, v - hi - mid], axis=0).astype(jnp.bfloat16)


def contrast(top_state, positive_keys, buffer, negative_slots):
    rows = top_state.shape[0]
    slots = buffer.shape[0]
    row_norm = jnp.sqrt(jnp.sum(top_state * top_state, axis=-1) + eps)
    unit_rows = top_state / row_norm[:, None]
    positive = positive_keys.astype(jnp.float32)
    positive_unit = positive / jnp.sqrt(jnp.sum(positive * positive, axis=-1, keepdims=True) + eps)
    positive_score = inverse_temp * jnp.sum(unit_rows * positive_unit, axis=-1)
    wide = buffer.astype(jnp.float32)
    key_scale = lax.rsqrt(jnp.sum(wide * wide, axis=-1) + eps)
    raw = lax.dot_general(
        split3(unit_rows), buffer, contract_last, preferred_element_type=jnp.float32
    )
    raw = raw[:rows] + raw[rows : 2 * rows] + raw[2 * rows :]
    scores = inverse_temp * raw * key_scale[None, :]
    slot_ids = lax.broadcasted_iota(jnp.int32, (1, 1, slots), 2)
    uses = jnp.sum((negative_slots[:, :, None] == slot_ids).astype(jnp.float32), axis=1)
    weights = jnp.where(uses > 0, uses * jnp.exp(scores), 0.0)
    positive_weight = jnp.exp(positive_score)
    exp_total = jnp.sum(weights, axis=-1) + positive_weight
    query_loss = jnp.log(exp_total) - positive_score
    coeffs = weights / exp_total[:, None]
    positive_coeff = positive_weight / exp_total - 1.0
    pull = lax.dot_general(
        split3(coeffs * key_scale[None, :]),
        buffer,
        (((1,), (0,)), ((), ())),
        preferred_element_type=jnp.float32,
    )
    pull = pull[:rows] + pull[rows : 2 * rows] + pull[2 * rows :]
    pull = inverse_temp * (pull + positive_coeff[:, None] * positive_unit)
    inner = jnp.sum(coeffs * scores, axis=-1) + positive_coeff * positive_score
    head_grad = ((pull - inner[:, None] * unit_rows) / row_norm[:, None]).astype(jnp.bfloat16)
    return (query_loss, head_grad)


def shards(
    mlp_input,
    residual_in,
    gate_weight,
    up_weight,
    down_weight,
    span_index,
    positive_keys,
    request_rows,
    request_counts,
    negative_slots,
):
    owners = lax.axis_size("dp") * lax.axis_size("fsdp")
    slot_cap = request_rows.shape[2]
    width = span_index.shape[1]
    row_table = request_rows[:, 0, :]
    live = lax.broadcasted_iota(jnp.int32, row_table.shape, 1) < request_counts
    wanted = jnp.where(live, row_table, -1).reshape(-1)
    pick = (wanted[:, None] == lax.broadcasted_iota(jnp.int32, (1, span_index.shape[0]), 1)).astype(
        jnp.bfloat16
    )
    picked = jnp.dot(pick, span_index, preferred_element_type=jnp.bfloat16)
    buffer = lax.all_to_all(
        picked.reshape(owners, slot_cap, width),
        ("dp", "fsdp"),
        split_axis=0,
        concat_axis=0,
        tiled=True,
    ).reshape(owners * slot_cap, width)
    whole_input = lax.all_gather(mlp_input, "fsdp", axis=1, tiled=True)
    gate_act = jnp.dot(whole_input, gate_weight, preferred_element_type=jnp.float32)
    up_act = jnp.dot(whole_input, up_weight, preferred_element_type=jnp.float32)
    sigmoid_gate = jax.nn.sigmoid(gate_act)
    silu_gate = gate_act * sigmoid_gate
    hidden = (silu_gate * up_act).astype(jnp.bfloat16)
    branch = lax.psum_scatter(
        jnp.dot(hidden, down_weight, preferred_element_type=jnp.float32).astype(jnp.bfloat16),
        "fsdp",
        scatter_dimension=0,
        tiled=True,
    ).astype(jnp.float32)
    top_state = branch + residual_in.astype(jnp.float32)
    all_hidden = lax.all_gather(hidden, "dp", axis=0, tiled=True)
    input_cols = lax.all_to_all(whole_input, "dp", split_axis=1, concat_axis=0, tiled=True)
    query_loss, head_grad = contrast(top_state, positive_keys, buffer, negative_slots)
    gathered_grad = lax.all_gather(head_grad, "fsdp", axis=0, tiled=True)
    hidden_grad = lax.dot_general(
        gathered_grad, down_weight, contract_last, preferred_element_type=jnp.float32
    )
    silu_slope = sigmoid_gate * (1.0 + gate_act * (1.0 - sigmoid_gate))
    gate_grad_act = (hidden_grad * up_act * silu_slope).astype(jnp.bfloat16)
    up_grad_act = (hidden_grad * silu_gate).astype(jnp.bfloat16)
    both_acts = lax.all_gather(
        jnp.concatenate([gate_grad_act, up_grad_act], axis=1), "dp", axis=0, tiled=True
    )
    input_term = lax.dot_general(
        gate_grad_act, gate_weight, contract_last, preferred_element_type=jnp.float32
    ) + lax.dot_general(up_grad_act, up_weight, contract_last, preferred_element_type=jnp.float32)
    input_grad = lax.psum_scatter(
        input_term.astype(jnp.bfloat16), "fsdp", scatter_dimension=1, tiled=True
    )
    head_cols = lax.all_to_all(gathered_grad, "dp", split_axis=1, concat_axis=0, tiled=True)
    down_grad = lax.dot_general(
        all_hidden, head_cols, contract_first, preferred_element_type=jnp.float32
    ).astype(jnp.bfloat16)
    units = gate_weight.shape[1]
    gate_grad = lax.dot_general(
        input_cols, both_acts[:, :units], contract_first, preferred_element_type=jnp.float32
    ).astype(jnp.bfloat16)
    up_grad = lax.dot_general(
        input_cols, both_acts[:, units:], contract_first, preferred_element_type=jnp.float32
    ).astype(jnp.bfloat16)
    return (query_loss, input_grad, gate_grad, up_grad, down_grad)


def solution(mesh):
    return jax.shard_map(
        shards,
        mesh=mesh,
        in_specs=(
            P("dp", "fsdp"),
            P(("dp", "fsdp"), None),
            P(None, "fsdp"),
            P(None, "fsdp"),
            P("fsdp", None),
            P(("dp", "fsdp"), None),
            P(("dp", "fsdp"), None),
            P(None, ("dp", "fsdp"), None),
            P(None, ("dp", "fsdp")),
            P(("dp", "fsdp"), None),
        ),
        out_specs=(
            P(("dp", "fsdp")),
            P("dp", "fsdp"),
            P("dp", "fsdp"),
            P("dp", "fsdp"),
            P("fsdp", "dp"),
        ),
        check_vma=False,
    )
```

profile of v0, /device:TPU:0, one launch (start us, length us, event | category | flops | bytes accessed | tf_op | source)
XLA Modules:
  0.0 431.6 jit_solution(6093604471115959801)
XLA Ops:
  10.6 9.0 %convolution_bitcast_fusion = bf16[128,8,4096]{2,1,0:T(8,128)(2,1)} fusion(bf16[512,4096]{1,0:T(8,128)(2,1)} %param.15, s32[1024]{0:T(1024)S(1)} %broadcast_select_fusion), kind=kOutput, calls=%fused_computation.5 | convolution fusion | flops 4295491584 | bytes 12587008 | tf_op jit(solution)/shard_map/dot_general | solution.py:75
  19.6 11.7 %all-to-all-start = ((bf16[128,8,4096]{2,1,0:T(8,128)(2,1)}), bf16[128,8,4096]{2,1,0:T(8,128)(2,1)}, u32[]{:S(2)}, u32[]{:S(2)}) async-start(bf16[128,8,4096]{2,1,0:T(8,128)(2,1)} %convolution_bitcast_fusion), calls=%async_computation.1 | async-start | bytes 16777216 | tf_op jit(solution)/shard_map/all_to_all | solution.py:76
  31.3 106.6 %all-gather.4.cloned.1.call-done = bf16[256,4096]{0,1:T(8,128)(2,1)} async-done(((bf16[256,128]{0,1:T(8,128)(2,1)}), bf16[256,4096]{0,1:T(8,128)(2,1)}) %all-gather.4.cloned.1.call-update) | async-done | bytes 2097168 | tf_op jit(solution)/shard_map/all_gather | solution.py:83
  137.9 4.0 fusion.36
  141.9 2.9 multiply_convert_fusion.2
  144.8 2.6 convolution_convert_fusion
  148.1 77.2 %reduce-scatter.5.cloned.1.call-done = bf16[8,4096]{1,0:T(8,128)(2,1)} async-done(((bf16[256,4096]{1,0:T(8,128)(2,1)}), bf16[8,4096]{1,0:T(8,128)(2,1)}) %reduce-scatter.5.cloned.1.call-update) | async-done | bytes 65552 | tf_op jit(solution)/shard_map/reduce_scatter | solution.py:89
  227.4 5.1 %multiply_reduce_fusion = f32[128,8]{1,0:T(8,128)S(1)} fusion(bf16[128,8,4096]{2,1,0:T(8,128)(2,1)} %all-to-all-done), kind=kLoop, calls=%fused_computation | loop fusion | flops 12581888 | bytes 8392704 | tf_op jit(solution)/shard_map/reduce_sum | solution.py:27
  232.7 5.7 %fusion.2 = f32[24,1024]{1,0:T(8,128)S(1)} fusion(bf16[128,8,4096]{2,1,0:T(8,128)(2,1)} %all-to-all-done, bf16[8,4096]{1,0:T(8,128)(2,1)S(1)} %get-tuple-element.16, bf16[8,4096]{1,0:T(8,128)(2,1)S(1)} %get-tuple-element.14, bf16[8,4096]{1,0:T(8,128)(2,1)S(1)} %get-tuple-element.13), kind=kOutput, calls=%fused_computation.3 | convolution fusion | flops 201916416 | bytes 8683520 | tf_op jit(solution)/shard_map/dot_general | solution.py:28
  239.2 4.6 %fusion = f32[24,4096]{1,0:T(8,128)S(1)} fusion(bf16[128,8,4096]{2,1,0:T(8,128)(2,1)} %all-to-all-done, bf16[8,1024]{1,0:T(8,128)(2,1)S(1)} %get-tuple-element.19, bf16[8,1024]{1,0:T(8,128)(2,1)S(1)} %get-tuple-element.18, bf16[8,1024]{1,0:T(8,128)(2,1)S(1)} %get-tuple-element.17), kind=kOutput, calls=%fused_computation.1 | convolution fusion | flops 201474048 | bytes 8830976 | tf_op jit(solution)/shard_map/dot_general | solution.py:41
  244.9 43.1 %all-gather.6.cloned.1.call-done = bf16[256,4096]{1,0:T(8,128)(2,1)} async-done(((bf16[8,4096]{1,0:T(8,128)(2,1)}), bf16[256,4096]{1,0:T(8,128)(2,1)}) %all-gather.6.cloned.1.call-update) | async-done | bytes 2097168 | tf_op jit(solution)/shard_map/all_gather | solution.py:99
  288.0 3.9 multiply_convert_fusion
  292.7 4.5 %all-to-all-start.1 = ((bf16[256,4,1024]{0,2,1:T(8,128)(2,1)}), bf16[256,4,1024]{0,2,1:T(8,128)(2,1)}, u32[]{:S(2)}, u32[]{:S(2)}) async-start(bf16[256,4,1024]{0,2,1:T(8,128)(2,1)} %bitcast.3), calls=%async_computation.2 | async-start | bytes 4194304 | tf_op jit(solution)/shard_map/all_to_all | solution.py:97
  297.2 3.5 fusion.35
  302.1 2.5 copy.29
  304.6 3.2 copy.33
  307.8 26.5 %all-to-all-done.1 = bf16[256,4,1024]{0,2,1:T(8,128)(2,1)} async-done(((bf16[256,4,1024]{0,2,1:T(8,128)(2,1)}), bf16[256,4,1024]{0,2,1:T(8,128)(2,1)}, u32[]{:S(2)}, u32[]{:S(2)}) %all-to-all-start.1) | async-done | bytes 2097184 | tf_op jit(solution)/shard_map/all_to_all | solution.py:97
  334.3 5.2 %all-to-all-start.2 = ((bf16[256,4,1024]{2,0,1:T(8,128)(2,1)}), bf16[256,4,1024]{2,0,1:T(8,128)(2,1)}, u32[]{:S(2)}, u32[]{:S(2)}) async-start(bf16[256,4,1024]{2,0,1:T(8,128)(2,1)} %bitcast.42), calls=%async_computation.3 | async-start | bytes 4194304 | tf_op jit(solution)/shard_map/all_to_all | solution.py:115
  339.4 35.8 %all_gather.15 = bf16[1024,448]{0,1:T(8,128)(2,1)S(1)} all-gather(bf16[256,448]{0,1:T(8,128)(2,1)S(1)} %get-tuple-element.21), channel_id=1, replica_groups=mesh['dp'=4,'fsdp'=32] {'dp'}, dimensions={0}, use_global_device_ids=true | all-gather | bytes 1146880 | tf_op jit(solution)/shard_map/all_gather | solution.py:96
  375.3 3.0 copy.27
  378.3 3.6 convolution_convert_fusion.1
  382.0 3.4 fusion.5
  385.3 2.1 fusion.6
  387.4 36.1 %reduce-scatter.7.cloned.1.call-done = bf16[128,256]{1,0:T(8,128)(2,1)} async-done(((bf16[4096,256]{1,0:T(8,128)(2,1)}), bf16[128,256]{1,0:T(8,128)(2,1)}) %reduce-scatter.7.cloned.1.call-update) | async-done | bytes 65552
  (53 shorter events, 12.0 us)
Async XLA Ops:
  7.2 130.7 %all-gather.4.cloned.1.call-start = ((), (), s32[]{:S(2)}) async-start(), calls=%async_computation.5 | async-start | bytes 2162688 | tf_op jit(solution)/shard_map/all_gather | solution.py:83
  19.6 207.9 %all-to-all-start = ((bf16[128,8,4096]{2,1,0:T(8,128)(2,1)}), bf16[128,8,4096]{2,1,0:T(8,128)(2,1)}, u32[]{:S(2)}, u32[]{:S(2)}) async-start(bf16[128,8,4096]{2,1,0:T(8,128)(2,1)} %convolution_bitcast_fusion), calls=%async_computation.1 | async-start | bytes 16777216 | tf_op jit(solution)/shard_map/all_to_all | solution.py:76
  31.3 194.1 %reduce-scatter.5.cloned.1.call-start = ((), (), s32[]{:S(2)}) async-start(), calls=%async_computation.6 | async-start | bytes 2162688 | tf_op jit(solution)/shard_map/reduce_scatter | solution.py:89
  137.9 4.0 copy-start.1
  141.9 2.9 copy-start
  144.8 2.7 copy-start.4
  144.8 2.9 copy-start.6
  144.8 80.6 %copy-start.3 = (bf16[8,4096]{1,0:T(8,128)(2,1)S(1)}, bf16[8,4096]{1,0:T(8,128)(2,1)}, u32[]{:S(2)}) copy-start(bf16[8,4096]{1,0:T(8,128)(2,1)} %param.11) | copy-start | bytes 196612
  147.5 140.5 %all-gather.6.cloned.1.call-start = ((), (), s32[]{:S(2)}) async-start(), calls=%async_computation.7 | async-start | bytes 2162688 | tf_op jit(solution)/shard_map/all_gather | solution.py:99
  239.2 4.6 %copy-start.5 = (bf16[8,4096]{1,0:T(8,128)(2,1)S(1)}, bf16[8,4096]{1,0:T(8,128)(2,1)}, u32[]{:S(2)}) copy-start(bf16[8,4096]{1,0:T(8,128)(2,1)} %reduce-scatter.5.cloned.1.call-done) | copy-start | bytes 196612
  244.6 137.3 %all-gather.8.cloned.1.call-start = ((), (), s32[]{:S(2)}) async-start(), calls=%async_computation.8 | async-start | bytes 2293760 | tf_op jit(solution)/shard_map/all_gather | solution.py:106
  292.7 41.6 %all-to-all-start.1 = ((bf16[256,4,1024]{0,2,1:T(8,128)(2,1)}), bf16[256,4,1024]{0,2,1:T(8,128)(2,1)}, u32[]{:S(2)}, u32[]{:S(2)}) async-start(bf16[256,4,1024]{0,2,1:T(8,128)(2,1)} %bitcast.3), calls=%async_computation.2 | async-start | bytes 4194304 | tf_op jit(solution)/shard_map/all_to_all | solution.py:97
  297.2 126.3 %reduce-scatter.7.cloned.1.call-start = ((), (), s32[]{:S(2)}) async-start(), calls=%async_computation.9 | async-start | bytes 2162688
  297.2 3.5 copy-start.2
  334.3 44.0 %all-to-all-start.2 = ((bf16[256,4,1024]{2,0,1:T(8,128)(2,1)}), bf16[256,4,1024]{2,0,1:T(8,128)(2,1)}, u32[]{:S(2)}, u32[]{:S(2)}) async-start(bf16[256,4,1024]{2,0,1:T(8,128)(2,1)} %bitcast.42), calls=%async_computation.3 | async-start | bytes 4194304 | tf_op jit(solution)/shard_map/all_to_all | solution.py:115
  382.0 3.4 copy-start.7
Sparse Core Ops, SparseCore 0:
  10.8 127.0 all-gather.3
  147.6 77.7 reduce-scatter.4
  244.8 43.1 all-gather.5
  292.8 46.3 all-gather.7
  342.5 80.8 reduce-scatter.6
where the time goes:
time: 432 us
  waiting for transfers between devices  290 us (67%)
  matrix products  46.6 us (11%)
  blocking collectives  35.8 us (8%)
  starting transfers between devices  21.7 us (5%)
  between operations  14 us (3%)
  local copies, waits for them, and re-layouts  12.9 us (3%)
  other arithmetic  11 us (3%)
    all_gather x1, waiting for transfers between devices, shards(): whole_input = lax.all_gather(mlp_input, 'fsdp', axis=1, tiled=True)  107 us
    reduce_scatter x1, waiting for transfers between devices, shards(): lax.psum_scatter(jnp.dot(hidden, down_weight, preferred_element_type=jnp....  77.2 us
    all_gather x1, waiting for transfers between devices, shards(): gathered_grad = lax.all_gather(head_grad, 'fsdp', axis=0, tiled=True)  43.1 us
    unnamed x6, waiting for transfers between devices  36.2 us
    all_gather x1, blocking collectives, shards(): all_hidden = lax.all_gather(hidden, 'dp', axis=0, tiled=True)  35.8 us
    all_to_all x1, waiting for transfers between devices, shards(): lax.all_to_all(whole_input, 'dp', split_axis=1, concat_axis=0, tiled=True)  26.5 us
    all_to_all x1, starting transfers between devices, shards(): lax.all_to_all(picked.reshape(owners, slot_cap, width), ('dp', 'fsdp'), s...  11.7 us
    dot_general x1, matrix products, shards(): picked = jnp.dot(pick, span_index, preferred_element_type=jnp.bfloat16)  9.02 us
  transfers between devices with their start and end apart: 8, of which 5 were waited for; matrix products, arithmetic and copies ran while one was open for 11% of the time, Pallas kernels for 0%

commit v1 on v0

--- a/solution.py
+++ b/solution.py
@@ -96,7 +96,15 @@
     all_hidden = lax.all_gather(hidden, "dp", axis=0, tiled=True)
     input_cols = lax.all_to_all(whole_input, "dp", split_axis=1, concat_axis=0, tiled=True)
     query_loss, head_grad = contrast(top_state, positive_keys, buffer, negative_slots)
-    gathered_grad = lax.all_gather(head_grad, "fsdp", axis=0, tiled=True)
+    gathered_grad = jnp.concatenate(
+        lax.all_to_all(
+            jnp.stack([head_grad] * lax.axis_size("fsdp")),
+            axis_name="fsdp",
+            split_axis=0,
+            concat_axis=0,
+        ),
+        axis=0,
+    )
     hidden_grad = lax.dot_general(
         gathered_grad, down_weight, contract_last, preferred_element_type=jnp.float32
     )

time: 432 us -> 419 us (0.970)
  waiting for transfers between devices: 290 us -> 239 us
  blocking collectives: 35.8 us -> 70.2 us
  local copies, waits for them, and re-layouts: 12.9 us -> 18.6 us
    all_gather x1 -> x0, waiting for transfers between devices: 43.1 us -> none  [shards(): gathered_grad = lax.all_gather(head_grad, 'fsdp', axis=0, tiled=True)]
    all_to_all x0 -> x1, blocking collectives: none -> 33.9 us  [shards(): lax.all_to_all(jnp.stack([head_grad] * lax.axis_size('fsdp')), axis_name=...]
    unnamed x6 -> x5, waiting for transfers between devices: 36.2 us -> 32.6 us
    unnamed x20 -> x26, local copies, waits for them, and re-layouts: 6.45 us -> 8.7 us
  transfers between devices with their start and end apart: 8 -> 7, of which waited for: 5 -> 4; matrix products, arithmetic and copies ran while one was open for 11% -> 11% of each run, Pallas kernels for 0% -> 0%
where the time goes in v1:
time: 419 us; the launch traced here: 418 us
  waiting for transfers between devices  239 us (57%)
  blocking collectives  70.2 us (17%)
  matrix products  44 us (11%)
  starting transfers between devices  21.1 us (5%)
  local copies, waits for them, and re-layouts  18.6 us (4%)
  between operations  14 us (3%)
  other arithmetic  10.4 us (2%)
    all_gather x1, waiting for transfers between devices, shards(): whole_input = lax.all_gather(mlp_input, 'fsdp', axis=1, tiled=True)  107 us
    reduce_scatter x1, waiting for transfers between devices, shards(): lax.psum_scatter(jnp.dot(hidden, down_weight, preferred_element_type=jnp....  76.5 us
    all_gather x1, blocking collectives, shards(): all_hidden = lax.all_gather(hidden, 'dp', axis=0, tiled=True)  36.4 us
    all_to_all x1, blocking collectives, shards(): lax.all_to_all(jnp.stack([head_grad] * lax.axis_size('fsdp')), axis_name=...  33.9 us
    unnamed x5, waiting for transfers between devices  32.6 us
    all_to_all x1, waiting for transfers between devices, shards(): lax.all_to_all(whole_input, 'dp', split_axis=1, concat_axis=0, tiled=True)  23.7 us
    all_to_all x1, starting transfers between devices, shards(): lax.all_to_all(picked.reshape(owners, slot_cap, width), ('dp', 'fsdp'), s...  11.7 us
    dot_general x1, matrix products, shards(): picked = jnp.dot(pick, span_index, preferred_element_type=jnp.bfloat16)  9.02 us
  transfers between devices with their start and end apart: 7, of which 4 were waited for; matrix products, arithmetic and copies ran while one was open for 11% of the time, Pallas kernels for 0%

profile of v1, /device:TPU:0, one launch (start us, length us, event | category | flops | bytes accessed | tf_op | source)
XLA Modules:
  0.0 417.6 jit_solution(5713844455338281506)
XLA Ops:
  10.6 9.0 %convolution_bitcast_fusion = bf16[128,8,4096]{2,1,0:T(8,128)(2,1)} fusion(bf16[512,4096]{1,0:T(8,128)(2,1)} %param.15, s32[1024]{0:T(1024)S(1)} %broadcast_select_fusion), kind=kOutput, calls=%fused_computation.5 | convolution fusion | flops 4295491584 | bytes 12587008 | tf_op jit(solution)/shard_map/dot_general | solution.py:75
  19.6 11.7 %all-to-all-start = ((bf16[128,8,4096]{2,1,0:T(8,128)(2,1)}), bf16[128,8,4096]{2,1,0:T(8,128)(2,1)}, u32[]{:S(2)}, u32[]{:S(2)}) async-start(bf16[128,8,4096]{2,1,0:T(8,128)(2,1)} %convolution_bitcast_fusion), calls=%async_computation.1 | async-start | bytes 16777216 | tf_op jit(solution)/shard_map/all_to_all | solution.py:76
  31.3 106.6 %all-gather.3.cloned.1.call-done = bf16[256,4096]{0,1:T(8,128)(2,1)} async-done(((bf16[256,128]{0,1:T(8,128)(2,1)}), bf16[256,4096]{0,1:T(8,128)(2,1)}) %all-gather.3.cloned.1.call-update) | async-done | bytes 2097168 | tf_op jit(solution)/shard_map/all_gather | solution.py:83
  137.9 4.0 fusion.38
  141.9 2.9 multiply_convert_fusion.2
  144.8 2.6 convolution_convert_fusion
  148.9 76.5 %reduce-scatter.5.cloned.1.call-done = bf16[8,4096]{1,0:T(8,128)(2,1)} async-done(((bf16[256,4096]{1,0:T(8,128)(2,1)}), bf16[8,4096]{1,0:T(8,128)(2,1)}) %reduce-scatter.5.cloned.1.call-update) | async-done | bytes 65552 | tf_op jit(solution)/shard_map/reduce_scatter | solution.py:89
  227.4 5.1 %multiply_reduce_fusion = f32[128,8]{1,0:T(8,128)S(1)} fusion(bf16[128,8,4096]{2,1,0:T(8,128)(2,1)} %all-to-all-done), kind=kLoop, calls=%fused_computation | loop fusion | flops 12581888 | bytes 8392704 | tf_op jit(solution)/shard_map/reduce_sum | solution.py:27
  232.6 5.7 %fusion.2 = f32[24,1024]{1,0:T(8,128)S(1)} fusion(bf16[128,8,4096]{2,1,0:T(8,128)(2,1)} %all-to-all-done, bf16[8,4096]{1,0:T(8,128)(2,1)S(1)} %get-tuple-element.16, bf16[8,4096]{1,0:T(8,128)(2,1)S(1)} %get-tuple-element.14, bf16[8,4096]{1,0:T(8,128)(2,1)S(1)} %get-tuple-element.13), kind=kOutput, calls=%fused_computation.3 | convolution fusion | flops 201916416 | bytes 8683520 | tf_op jit(solution)/shard_map/dot_general | solution.py:28
  239.2 4.6 %fusion = f32[24,4096]{1,0:T(8,128)S(1)} fusion(bf16[128,8,4096]{2,1,0:T(8,128)(2,1)} %all-to-all-done, bf16[8,1024]{1,0:T(8,128)(2,1)S(1)} %get-tuple-element.19, bf16[8,1024]{1,0:T(8,128)(2,1)S(1)} %get-tuple-element.18, bf16[8,1024]{1,0:T(8,128)(2,1)S(1)} %get-tuple-element.17), kind=kOutput, calls=%fused_computation.1 | convolution fusion | flops 201474048 | bytes 8830976 | tf_op jit(solution)/shard_map/dot_general | solution.py:41
  244.2 33.9 %all_to_all.48 = bf16[32,8,4096]{2,1,0:T(8,128)(2,1)S(1)} all-to-all(bf16[32,8,4096]{2,1,0:T(8,128)(2,1)S(1)} %stack.2), channel_id=1, replica_groups=mesh['dp'=4,'fsdp'=32] {'fsdp'}, dimensions={0} | all-to-all | bytes 4194304 | tf_op jit(solution)/shard_map/all_to_all | solution.py:100
  280.2 4.5 %all-to-all-start.2 = ((bf16[256,4,1024]{0,2,1:T(8,128)(2,1)}), bf16[256,4,1024]{0,2,1:T(8,128)(2,1)}, u32[]{:S(2)}, u32[]{:S(2)}) async-start(bf16[256,4,1024]{0,2,1:T(8,128)(2,1)} %bitcast.4), calls=%async_computation.3 | async-start | bytes 4194304 | tf_op jit(solution)/shard_map/all_to_all | solution.py:97
  284.7 3.6 fusion.37
  289.7 2.5 copy.28
  293.8 2.8 all_to_all.40
  296.6 3.5 copy.27
  300.1 23.7 %all-to-all-done.2 = bf16[256,4,1024]{0,2,1:T(8,128)(2,1)} async-done(((bf16[256,4,1024]{0,2,1:T(8,128)(2,1)}), bf16[256,4,1024]{0,2,1:T(8,128)(2,1)}, u32[]{:S(2)}, u32[]{:S(2)}) %all-to-all-start.2) | async-done | bytes 2097184 | tf_op jit(solution)/shard_map/all_to_all | solution.py:97
  323.9 4.6 %all-to-all-start.3 = ((bf16[256,4,1024]{2,0,1:T(8,128)(2,1)}), bf16[256,4,1024]{2,0,1:T(8,128)(2,1)}, u32[]{:S(2)}, u32[]{:S(2)}) async-start(bf16[256,4,1024]{2,0,1:T(8,128)(2,1)} %copy.27), calls=%async_computation.4 | async-start | bytes 4194304 | tf_op jit(solution)/shard_map/all_to_all | solution.py:123
  328.5 36.4 %all_gather.11 = bf16[1024,448]{0,1:T(8,128)(2,1)S(1)} all-gather(bf16[256,448]{0,1:T(8,128)(2,1)S(1)} %get-tuple-element.21), channel_id=1, replica_groups=mesh['dp'=4,'fsdp'=32] {'dp'}, dimensions={0}, use_global_device_ids=true | all-gather | bytes 1146880 | tf_op jit(solution)/shard_map/all_gather | solution.py:96
  364.9 3.0 copy.26
  367.9 3.6 convolution_convert_fusion.1
  371.5 3.4 fusion.7
  374.9 2.1 fusion.8
  376.9 32.5 %reduce-scatter.7.cloned.1.call-done = bf16[128,256]{1,0:T(8,128)(2,1)} async-done(((bf16[4096,256]{1,0:T(8,128)(2,1)}), bf16[128,256]{1,0:T(8,128)(2,1)}) %reduce-scatter.7.cloned.1.call-update) | async-done | bytes 65552
  (59 shorter events, 15.0 us)
Async XLA Ops:
  7.2 130.7 %all-gather.3.cloned.1.call-start = ((), (), s32[]{:S(2)}) async-start(), calls=%async_computation.6 | async-start | bytes 2162688 | tf_op jit(solution)/shard_map/all_gather | solution.py:83
  19.6 207.8 %all-to-all-start = ((bf16[128,8,4096]{2,1,0:T(8,128)(2,1)}), bf16[128,8,4096]{2,1,0:T(8,128)(2,1)}, u32[]{:S(2)}, u32[]{:S(2)}) async-start(bf16[128,8,4096]{2,1,0:T(8,128)(2,1)} %convolution_bitcast_fusion), calls=%async_computation.1 | async-start | bytes 16777216 | tf_op jit(solution)/shard_map/all_to_all | solution.py:76
  31.3 194.1 %reduce-scatter.5.cloned.1.call-start = ((), (), s32[]{:S(2)}) async-start(), calls=%async_computation.7 | async-start | bytes 2162688 | tf_op jit(solution)/shard_map/reduce_scatter | solution.py:89
  137.9 4.0 copy-start.4
  141.9 2.9 copy-start.2
  147.4 0.8 copy-start.7
  147.4 1.0 copy-start.9
  147.4 77.9 %copy-start.6 = (bf16[8,4096]{1,0:T(8,128)(2,1)S(1)}, bf16[8,4096]{1,0:T(8,128)(2,1)}, u32[]{:S(2)}) copy-start(bf16[8,4096]{1,0:T(8,128)(2,1)} %param.11) | copy-start | bytes 196612
  147.4 224.1 %all-gather.5.cloned.1.call-start = ((), (), s32[]{:S(2)}) async-start(), calls=%async_computation.8 | async-start | bytes 2293760 | tf_op jit(solution)/shard_map/all_gather | solution.py:114
  239.2 4.6 %copy-start.8 = (bf16[8,4096]{1,0:T(8,128)(2,1)S(1)}, bf16[8,4096]{1,0:T(8,128)(2,1)}, u32[]{:S(2)}) copy-start(bf16[8,4096]{1,0:T(8,128)(2,1)} %reduce-scatter.5.cloned.1.call-done) | copy-start | bytes 196612
  244.2 33.9 %copy-start.3 = (bf16[448,4096]{1,0:T(8,128)(2,1)S(1)}, bf16[448,4096]{1,0:T(8,128)(2,1)}, u32[]{:S(2)}) copy-start(bf16[448,4096]{1,0:T(8,128)(2,1)} %param.14) | copy-start | bytes 11010052
  278.1 1.3 copy-start
  280.2 43.7 %all-to-all-start.2 = ((bf16[256,4,1024]{0,2,1:T(8,128)(2,1)}), bf16[256,4,1024]{0,2,1:T(8,128)(2,1)}, u32[]{:S(2)}, u32[]{:S(2)}) async-start(bf16[256,4,1024]{0,2,1:T(8,128)(2,1)} %bitcast.4), calls=%async_computation.3 | async-start | bytes 4194304 | tf_op jit(solution)/shard_map/all_to_all | solution.py:97
  284.7 124.8 %reduce-scatter.7.cloned.1.call-start = ((), (), s32[]{:S(2)}) async-start(), calls=%async_computation.9 | async-start | bytes 2162688
  284.7 3.6 copy-start.5
  292.2 1.6 copy-start.1
  323.9 44.0 %all-to-all-start.3 = ((bf16[256,4,1024]{2,0,1:T(8,128)(2,1)}), bf16[256,4,1024]{2,0,1:T(8,128)(2,1)}, u32[]{:S(2)}, u32[]{:S(2)}) async-start(bf16[256,4,1024]{2,0,1:T(8,128)(2,1)} %copy.27), calls=%async_computation.4 | async-start | bytes 4194304 | tf_op jit(solution)/shard_map/all_to_all | solution.py:123
  371.5 3.4 copy-start.10
Sparse Core Ops, SparseCore 0:
  10.8 127.0 all-gather.2
  147.6 77.7 reduce-scatter.4
  280.3 46.1 all-gather.4
  329.9 79.5 reduce-scatter.6
